TPU v7x, 32 devices: a whole 2x2x4 slice. The times are simulated.
32 devices in a mesh: state: 8 (over z, y), mem: 4 (over x, core).
Axes of the slice: x: 2, y: 2, z: 4, core: 2. Of those that a mesh axis runs over, the one named last changes fastest.
Arguments:
- background_matrix: float32 [80, 524288], P('mem', 'state'), may hold values from -6 to 6
- measured_readings: float32 [4, 192], replicated, may hold values from -8 to 8
- measurement_noise: float32 [4, 192], replicated, may hold values from 0.5 to 2
- holding_processor: int32 [4], replicated, may hold values from 0 to 31
- measured_position: int32 [4, 192], replicated, may hold values from 0 to 16383
- taper_grade: int32 [4, 192, 1024], P(None, None, ('state', 'mem')), may hold values from 0 to 4
Outputs:
- analysis: float32 [80, 524288], P(None, ('state', 'mem'))
Inputs may be any that keep to these rules, and one draw needn't show every extreme that they name: `holding_processor`: batches may share an owner; observations of a batch may share a variable.
All inputs are finite; a program needn't handle non-finite values.
Results may differ from a plain program's by a relative error of at most 0.0003.
Values sent between devices are 32-bit elements; how exact they have to be, the bound alone decides.
No kernel may reach another device: no remote copies, remote signals or barrier semaphores. Data moves between devices by JAX's collectives and lax.ppermute only.
A program may use at most 256 MiB of HBM per device.

v0:
```python
import jax
import jax.numpy as jnp
from jax import lax
from jax.sharding import PartitionSpec as P

BATCHES = 4


PRECISE = lax.Precision.HIGHEST


def broadcast(block, axis, source):
    block = jnp.where(lax.axis_index(axis) == source, block, jnp.zeros_like(block))
    return lax.psum(block, axis)


def system_inverse(prior, errors):
    spread = prior - jnp.mean(prior, axis=0)
    system = jnp.dot(spread.T, spread, precision=PRECISE) / (prior.shape[0] - 1) + jnp.diag(errors)
    factor = jnp.linalg.cholesky(system)
    identity = jnp.eye(system.shape[0], dtype=system.dtype)
    lower_inv = lax.linalg.triangular_solve(factor, identity, left_side=True, lower=True)
    return jnp.dot(lower_inv.T, lower_inv, precision=PRECISE)


def expand_levels(levels, block_width):
    scaled = levels.astype(jnp.float32) / 4.0
    widened = scaled[:, :, None] * jnp.ones((block_width,), jnp.float32)
    return widened.reshape(levels.shape[0], levels.shape[1] * block_width)


def update_columns(realization_slab, taper, spread, innovation, inverse):
    center = jnp.mean(realization_slab, axis=0, keepdims=True)
    anomaly = realization_slab - center
    cov = jnp.dot(spread.T, anomaly, precision=PRECISE) / (realization_slab.shape[0] - 1)
    weights = jnp.dot(inverse, taper * cov, precision=PRECISE)
    center = center + jnp.dot(innovation[None, :], weights, precision=PRECISE)
    anomaly = anomaly - 0.5 * jnp.dot(spread, weights, precision=PRECISE)
    return center + anomaly


def announce(prior, root, errors):
    shared = broadcast(prior, ("state", "mem"), root)
    return (shared, system_inverse(shared, errors))


def local(
    background_matrix,
    measured_readings,
    measurement_noise,
    holding_processor,
    measured_position,
    taper_grade,
):
    realization_slab = lax.all_to_all(
        background_matrix, "mem", split_axis=1, concat_axis=0, tiled=True
    )
    block_width = realization_slab.shape[1] // taper_grade.shape[2]
    shared, inverse = announce(
        jnp.take(realization_slab, measured_position[0], axis=1),
        holding_processor[0],
        measurement_noise[0],
    )
    for batch in range(BATCHES):
        center = jnp.mean(shared, axis=0)
        spread = shared - center
        innovation = measured_readings[batch] - center
        taper = expand_levels(taper_grade[batch], block_width)
        if batch + 1 < BATCHES:
            realization_slab = update_columns(realization_slab, taper, spread, innovation, inverse)
            next_prior = jnp.take(realization_slab, measured_position[batch + 1], axis=1)
            shared, inverse = announce(
                next_prior, holding_processor[batch + 1], measurement_noise[batch + 1]
            )
        else:
            realization_slab = update_columns(realization_slab, taper, spread, innovation, inverse)
    return realization_slab


def solution(mesh):
    return jax.shard_map(
        local,
        mesh=mesh,
        in_specs=(P("mem", "state"), P(), P(), P(), P(), P(None, None, ("state", "mem"))),
        out_specs=P(None, ("state", "mem")),
        check_vma=False,
    )
```

profile of v0, /device:TPU:0, one launch (start us, length us, event | category | flops | bytes accessed | tf_op | source)
XLA Modules:
  0.0 761.5 jit_solution(15877180458151621214)
XLA Ops:
  0.0 7.1 all_to_all.14
  7.1 8.1 %copy.24 = f32[20,4,16384]{2,0,1:T(8,128)} copy(f32[20,4,16384]{2,1,0:T(4,128)} %all_to_all.14) | data formatting | bytes 10485760 | tf_op jit(solution)/shard_map/all_to_all | solution.py:55
  15.2 5.5 all-to-all-start
  25.7 20.4 %copy.45 = f32[24,8,32,512]{3,1,2,0:T(8,128)} copy(f32[24,8,32,512]{3,2,1,0:T(8,128)} %bitcast.185) | data formatting | bytes 25165824
  48.2 5.3 mul.54
  53.5 20.6 %copy.46 = f32[24,8,32,512]{3,1,2,0:T(8,128)} copy(f32[24,8,32,512]{3,2,1,0:T(8,128)} %bitcast.186) | data formatting | bytes 25165824
  79.9 20.4 %copy.47 = f32[24,8,32,512]{3,1,2,0:T(8,128)} copy(f32[24,8,32,512]{3,2,1,0:T(8,128)} %bitcast.187) | data formatting | bytes 25165824
  106.3 20.6 %copy.48 = f32[24,8,32,512]{3,1,2,0:T(8,128)} copy(f32[24,8,32,512]{3,2,1,0:T(8,128)} %bitcast.188) | data formatting | bytes 25165824
  131.8 7.9 %copy.25 = f32[80,16384]{0,1:T(8,128)} copy(f32[80,16384]{1,0:T(8,128)} %all_to_all.17) | data formatting | bytes 10485760 | tf_op jit(solution)/shard_map/all_to_all | solution.py:55
  143.9 43.6 %psum.28 = f32[80,192]{0,1:T(8,128)S(1)} all-reduce(f32[80,192]{0,1:T(8,128)S(1)} %bitcast_select_fusion.3), channel_id=1, replica_groups=mesh['state'=8,'mem'=4] {'state','mem'}, use_global_device_ids=true, to_apply=%region_1.3 | all-reduce | flops 15360 | bytes 122880 | tf_op jit(solution)/shard_map/psum | solution.py:14
  188.2 11.7 %cholesky.228 = f32[128,128]{1,0:T(8,128)S(1)} custom-call(f32[128,128]{1,0:T(8,128)S(1)} %cholesky.376), custom_call_target="Cholesky" | custom-call | tf_op jit(solution)/shard_map/jit(cholesky)/cholesky | solution.py:20
  199.9 9.8 %custom-call.17 = f32[1,128,128]{1,2,0:T(8,128)S(1)} custom-call(f32[1,128,128]{2,1,0:T(8,128)S(1)} %get-tuple-element.57), custom_call_target="InvertDiagBlocksLowerTriangular" | custom-call | tf_op jit(solution)/shard_map/jit(cholesky)/cholesky | solution.py:20
  210.1 5.8 cholesky.248
  218.8 19.7 %custom-call.18 = f32[2,128,128]{1,2,0:T(8,128)S(1)} custom-call(f32[2,128,128]{2,1,0:T(8,128)S(1)} %pad_maximum_fusion), custom_call_target="InvertDiagBlocksLowerTriangular" | custom-call | tf_op jit(solution)/shard_map/triangular_solve/custom-call.0 | solution.py:22
  242.8 18.8 %fusion.3 = f32[192,16384]{1,0:T(8,128)} fusion(f32[192,16384]{1,0:T(8,128)} %bitcast.192, f32[80,16384]{1,0:T(8,128)} %all_to_all.17, f32[16384]{0:T(1024)S(1)} %broadcast_multiply_fusion.3, f32[80,192]{0,1:T(8,128)S(1)} %psum.28, f32[192]{0:T(256)S(1)} %broadcast_multiply_fusion.7), kind=kOutput, calls=%fused_computation.11 | convolution fusion | flops 3027516416 | bytes 30536448 | tf_op jit(solution)/shard_map/dot_general | solution.py:35
  261.6 15.5 %fusion.131 = f32[192,16384]{1,0:T(8,128)S(1)} fusion(f32[192,192]{1,0:T(8,128)S(1)} %fusion.24, f32[192,16384]{1,0:T(8,128)} %fusion.3), kind=kOutput, calls=%fused_computation.247 | convolution fusion | flops 7247757312 | bytes 25313280 | tf_op jit(solution)/shard_map/dot_general | solution.py:36
  277.2 6.0 fusion.107
  283.2 10.4 %fusion.128 = (f32[16384]{0:T(1024)S(1)}, f32[80,16384]{1,0:T(8,128)}) fusion(f32[192,16384]{1,0:T(8,128)S(1)} %fusion.131, f32[80,192]{0,1:T(8,128)S(1)} %psum.28, f32[192]{0:T(256)S(1)} %broadcast_multiply_fusion.7, f32[80,16384]{1,0:T(8,128)S(1)} %bitcast.184, f32[16384]{0:T(1024)S(1)} %broadcast_multiply_fusion.3, f32[16384]{0:T(1024)S(1)} %fusion.121), kind=kOutput, calls=%fused_computation.244 | convolution fusion | flops 3026451456 | bytes 23327488 | tf_op jit(solution)/shard_map/dot_general | solution.py:38
  293.7 7.9 %copy.29 = f32[80,16384]{0,1:T(8,128)} copy(f32[80,16384]{1,0:T(8,128)} %get-tuple-element.83) | data formatting | bytes 10485760 | tf_op jit(solution)/shard_map/add | solution.py:39
  305.7 41.0 %psum.29 = f32[80,192]{0,1:T(8,128)S(1)} all-reduce(f32[80,192]{0,1:T(8,128)S(1)} %bitcast_select_fusion.2), channel_id=1, replica_groups=mesh['state'=8,'mem'=4] {'state','mem'}, use_global_device_ids=true, to_apply=%region_8.12 | all-reduce | flops 15360 | bytes 122880 | tf_op jit(solution)/shard_map/psum | solution.py:14
  347.4 11.7 %cholesky.266 = f32[128,128]{1,0:T(8,128)S(1)} custom-call(f32[128,128]{1,0:T(8,128)S(1)} %cholesky.379), custom_call_target="Cholesky" | custom-call | tf_op jit(solution)/shard_map/jit(cholesky)/cholesky | solution.py:20
  359.2 9.8 %custom-call.19 = f32[1,128,128]{1,2,0:T(8,128)S(1)} custom-call(f32[1,128,128]{2,1,0:T(8,128)S(1)} %get-tuple-element.55), custom_call_target="InvertDiagBlocksLowerTriangular" | custom-call | tf_op jit(solution)/shard_map/jit(cholesky)/cholesky | solution.py:20
  369.4 5.8 cholesky.286
  377.9 19.7 %custom-call.20 = f32[2,128,128]{1,2,0:T(8,128)S(1)} custom-call(f32[2,128,128]{2,1,0:T(8,128)S(1)} %pad_maximum_fusion.1), custom_call_target="InvertDiagBlocksLowerTriangular" | custom-call | tf_op jit(solution)/shard_map/triangular_solve/custom-call.0 | solution.py:22
  398.7 18.8 %fusion.2 = f32[192,16384]{1,0:T(8,128)} fusion(f32[192,16384]{1,0:T(8,128)} %bitcast.191, f32[80,16384]{1,0:T(8,128)} %get-tuple-element.83, f32[16384]{0:T(1024)S(1)} %broadcast_multiply_fusion.2, f32[80,192]{0,1:T(8,128)S(1)} %psum.29, f32[192]{0:T(256)S(1)} %broadcast_multiply_fusion.6), kind=kOutput, calls=%fused_computation.9 | convolution fusion | flops 3027516416 | bytes 30536448 | tf_op jit(solution)/shard_map/dot_general | solution.py:35
  417.5 15.5 %fusion.132 = f32[192,16384]{1,0:T(8,128)S(1)} fusion(f32[192,192]{1,0:T(8,128)S(1)} %fusion.28, f32[192,16384]{1,0:T(8,128)} %fusion.2), kind=kOutput, calls=%fused_computation.248 | convolution fusion | flops 7247757312 | bytes 25313280 | tf_op jit(solution)/shard_map/dot_general | solution.py:36
  433.0 6.0 fusion.105
  439.1 10.4 %fusion.129 = (f32[16384]{0:T(1024)S(1)}, f32[80,16384]{1,0:T(8,128)}) fusion(f32[192,16384]{1,0:T(8,128)S(1)} %fusion.132, f32[80,192]{0,1:T(8,128)S(1)} %psum.29, f32[192]{0:T(256)S(1)} %broadcast_multiply_fusion.6, f32[80,16384]{1,0:T(8,128)S(1)} %bitcast.180, f32[16384]{0:T(1024)S(1)} %broadcast_multiply_fusion.2, f32[16384]{0:T(1024)S(1)} %fusion.122), kind=kOutput, calls=%fused_computation.245 | convolution fusion | flops 3026451456 | bytes 23327488 | tf_op jit(solution)/shard_map/dot_general | solution.py:38
  449.5 7.9 %copy.33 = f32[80,16384]{0,1:T(8,128)} copy(f32[80,16384]{1,0:T(8,128)} %get-tuple-element.87) | data formatting | bytes 10485760 | tf_op jit(solution)/shard_map/add | solution.py:39
  461.6 41.0 %psum.30 = f32[80,192]{0,1:T(8,128)S(1)} all-reduce(f32[80,192]{0,1:T(8,128)S(1)} %bitcast_select_fusion.1), channel_id=1, replica_groups=mesh['state'=8,'mem'=4] {'state','mem'}, use_global_device_ids=true, to_apply=%region_11.15 | all-reduce | flops 15360 | bytes 122880 | tf_op jit(solution)/shard_map/psum | solution.py:14
  503.3 11.7 %cholesky.304 = f32[128,128]{1,0:T(8,128)S(1)} custom-call(f32[128,128]{1,0:T(8,128)S(1)} %cholesky.382), custom_call_target="Cholesky" | custom-call | tf_op jit(solution)/shard_map/jit(cholesky)/cholesky | solution.py:20
  515.0 9.8 %custom-call.21 = f32[1,128,128]{1,2,0:T(8,128)S(1)} custom-call(f32[1,128,128]{2,1,0:T(8,128)S(1)} %get-tuple-element.53), custom_call_target="InvertDiagBlocksLowerTriangular" | custom-call | tf_op jit(solution)/shard_map/jit(cholesky)/cholesky | solution.py:20
  525.2 5.8 cholesky.324
  533.8 19.7 %custom-call.22 = f32[2,128,128]{1,2,0:T(8,128)S(1)} custom-call(f32[2,128,128]{2,1,0:T(8,128)S(1)} %pad_maximum_fusion.2), custom_call_target="InvertDiagBlocksLowerTriangular" | custom-call | tf_op jit(solution)/shard_map/triangular_solve/custom-call.0 | solution.py:22
  554.5 18.9 %fusion.1 = f32[192,16384]{1,0:T(8,128)} fusion(f32[192,16384]{1,0:T(8,128)} %bitcast.190, f32[80,16384]{1,0:T(8,128)} %get-tuple-element.87, f32[16384]{0:T(1024)S(1)} %broadcast_multiply_fusion.1, f32[80,192]{0,1:T(8,128)S(1)} %psum.30, f32[192]{0:T(256)S(1)} %broadcast_multiply_fusion.5), kind=kOutput, calls=%fused_computation.7 | convolution fusion | flops 3027516416 | bytes 30536448 | tf_op jit(solution)/shard_map/dot_general | solution.py:35
  573.5 15.5 %fusion.133 = f32[192,16384]{1,0:T(8,128)S(1)} fusion(f32[192,192]{1,0:T(8,128)S(1)} %fusion.32, f32[192,16384]{1,0:T(8,128)} %fusion.1), kind=kOutput, calls=%fused_computation.249 | convolution fusion | flops 7247757312 | bytes 25313280 | tf_op jit(solution)/shard_map/dot_general | solution.py:36
  589.0 6.0 fusion.103
  595.0 10.4 %fusion.130 = (f32[16384]{0:T(1024)S(1)}, f32[80,16384]{1,0:T(8,128)}) fusion(f32[192,16384]{1,0:T(8,128)S(1)} %fusion.133, f32[80,192]{0,1:T(8,128)S(1)} %psum.30, f32[192]{0:T(256)S(1)} %broadcast_multiply_fusion.5, f32[80,16384]{1,0:T(8,128)S(1)} %bitcast.182, f32[16384]{0:T(1024)S(1)} %broadcast_multiply_fusion.1, f32[16384]{0:T(1024)S(1)} %fusion.123), kind=kOutput, calls=%fused_computation.246 | convolution fusion | flops 3026451456 | bytes 23327488 | tf_op jit(solution)/shard_map/dot_general | solution.py:38
  605.5 7.9 %copy.37 = f32[80,16384]{0,1:T(8,128)} copy(f32[80,16384]{1,0:T(8,128)} %get-tuple-element.91) | data formatting | bytes 10485760 | tf_op jit(solution)/shard_map/add | solution.py:39
  617.5 40.9 %psum.31 = f32[80,192]{0,1:T(8,128)S(1)} all-reduce(f32[80,192]{0,1:T(8,128)S(1)} %bitcast_select_fusion), channel_id=1, replica_groups=mesh['state'=8,'mem'=4] {'state','mem'}, use_global_device_ids=true, to_apply=%region_14.18 | all-reduce | flops 15360 | bytes 122880 | tf_op jit(solution)/shard_map/psum | solution.py:14
  659.2 11.7 %cholesky.342 = f32[128,128]{1,0:T(8,128)S(1)} custom-call(f32[128,128]{1,0:T(8,128)S(1)} %cholesky.385), custom_call_target="Cholesky" | custom-call | tf_op jit(solution)/shard_map/jit(cholesky)/cholesky | solution.py:20
  671.0 9.8 %custom-call.23 = f32[1,128,128]{1,2,0:T(8,128)S(1)} custom-call(f32[1,128,128]{2,1,0:T(8,128)S(1)} %get-tuple-element.51), custom_call_target="InvertDiagBlocksLowerTriangular" | custom-call | tf_op jit(solution)/shard_map/jit(cholesky)/cholesky | solution.py:20
  681.2 5.8 cholesky.362
  689.9 19.7 %custom-call.24 = f32[2,128,128]{1,2,0:T(8,128)S(1)} custom-call(f32[2,128,128]{2,1,0:T(8,128)S(1)} %pad_maximum_fusion.3), custom_call_target="InvertDiagBlocksLowerTriangular" | custom-call | tf_op jit(solution)/shard_map/triangular_solve/custom-call.0 | solution.py:22
  710.6 18.8 %fusion = f32[192,16384]{1,0:T(8,128)} fusion(f32[192,16384]{1,0:T(8,128)} %bitcast.189, f32[80,16384]{1,0:T(8,128)} %get-tuple-element.91, f32[16384]{0:T(1024)S(1)} %broadcast_multiply_fusion, f32[80,192]{0,1:T(8,128)S(1)} %psum.31, f32[192]{0:T(256)S(1)} %broadcast_multiply_fusion.4), kind=kOutput, calls=%fused_computation.5 | convolution fusion | flops 3027516416 | bytes 30536448 | tf_op jit(solution)/shard_map/dot_general | solution.py:35
  729.5 15.4 %fusion.134 = f32[192,16384]{1,0:T(8,128)S(1)} fusion(f32[192,192]{1,0:T(8,128)S(1)} %fusion.36, f32[192,16384]{1,0:T(8,128)} %fusion), kind=kOutput, calls=%fused_computation.250 | convolution fusion | flops 7247757312 | bytes 25313280 | tf_op jit(solution)/shard_map/dot_general | solution.py:36
  744.8 6.0 fusion.101
  750.9 10.1 %fusion.5 = f32[80,16384]{1,0:T(8,128)} fusion(f32[192,16384]{1,0:T(8,128)S(1)} %fusion.134, f32[80,16384]{1,0:T(8,128)S(1)} %bitcast.178, f32[16384]{0:T(1024)S(1)} %fusion.124, f32[16384]{0:T(1024)S(1)} %broadcast_multiply_fusion, f32[80,192]{0,1:T(8,128)S(1)} %psum.31, f32[192]{0:T(256)S(1)} %broadcast_multiply_fusion.4), kind=kOutput, calls=%fused_computation.14 | convolution fusion | flops 3025157120 | bytes 23261952 | tf_op jit(solution)/shard_map/dot_general | solution.py:38
  (161 shorter events, 55.5 us)
Async XLA Ops:
  7.1 13.6 %copy-start = (s32[4,192,32]{1,2,0:T(8,128)S(1)}, s32[4,192,32]{1,2,0:T(8,128)}, u32[]{:S(2)}) copy-start(s32[4,192,32]{1,2,0:T(8,128)} %param.16) | copy-start | bytes 294916
  15.2 111.9 %all-to-all-start = ((f32[20,4,16384]{2,0,1:T(8,128)}), f32[20,4,16384]{2,0,1:T(8,128)}, u32[]{:S(2)}, u32[]{:S(2)}) async-start(f32[20,4,16384]{2,0,1:T(8,128)} %copy.24), calls=%async_computation | async-start | bytes 12582912 | tf_op jit(solution)/shard_map/all_to_all | solution.py:55
  25.7 20.4 %copy-start.2 = (s32[4]{0:T(128)S(1)}, s32[4]{0:T(128)}, u32[]{:S(2)}) copy-start(s32[4]{0:T(128)} %param.14) | copy-start | bytes 52
  106.3 20.6 %copy-start.3 = (s32[4,192]{1,0:T(4,128)S(1)}, s32[4,192]{1,0:T(4,128)}, u32[]{:S(2)}) copy-start(s32[4,192]{1,0:T(4,128)} %param.15) | copy-start | bytes 9220
  106.3 20.8 %copy-start.4 = (f32[4,192]{1,0:T(4,128)S(1)}, f32[4,192]{1,0:T(4,128)}, u32[]{:S(2)}) copy-start(f32[4,192]{1,0:T(4,128)} %param.13) | copy-start | bytes 9220
  261.6 15.5 %copy-start.1 = (f32[4,192]{1,0:T(4,128)S(1)}, f32[4,192]{1,0:T(4,128)}, u32[]{:S(2)}) copy-start(f32[4,192]{1,0:T(4,128)} %param.12) | copy-start | bytes 9220
  277.2 6.0 slice-start.6
  277.2 6.0 slice-start.7
  433.0 6.0 slice-start.2
  433.0 6.0 slice-start.3
  589.0 6.0 slice-start.4
  589.0 6.0 slice-start.5
  744.8 6.0 slice-start
  744.8 6.0 slice-start.1
where the time goes:
time: 767 us; the launch traced here: 761 us
  matrix products  210 us (27%)
  other arithmetic  198 us (26%)
  local copies, waits for them, and re-layouts  172 us (22%)
  blocking collectives  166 us (22%)
  between operations  9.04 us (1%)
    psum x4, blocking collectives, broadcast(): return lax.psum(block, axis)  166 us
    another operation x28, other arithmetic, system_inverse(): factor = jnp.linalg.cholesky(system)  115 us
    unnamed x30, local copies, waits for them, and re-layouts  82.1 us
    another operation x18, other arithmetic, system_inverse(): lax.linalg.triangular_solve(factor, identity, left_side=True, lower=True)  79.2 us
    dot_general x4, matrix products, update_columns(): jnp.dot(spread.T, anomaly, precision=PRECISE)  75.4 us
    dot_general x4, matrix products, update_columns(): weights = jnp.dot(inverse, taper * cov, precision=PRECISE)  61.9 us
    dot_general x4, matrix products, update_columns(): anomaly = anomaly - 0.5 * jnp.dot(spread, weights, precision=PRECISE)  41.4 us
    all_to_all x4, local copies, waits for them, and re-layouts, local(): lax.all_to_all(background_matrix, 'mem', split_axis=1, concat_axis=0, til...  27.8 us
  transfers between devices with their start and end apart: 1, of which 0 were waited for; matrix products, arithmetic and copies ran while one was open for 14% of the time, Pallas kernels for 0%

commit v1 on v0

v1 whole, which is shorter than its diff:
```python
import functools

import jax
import jax.numpy as jnp
from jax import lax
from jax.experimental import pallas as pl
from jax.experimental.pallas import tpu as pltpu
from jax.sharding import PartitionSpec as P

LANES = 128
SUBLANES = 8
EXACT = lax.Precision.HIGHEST
NN = (((1,), (0,)), ((), ()))
NT = (((1,), (1,)), ((), ()))
TN = (((0,), (0,)), ((), ()))
VMEM_LIMIT = 56 * 1024 * 1024


def dot32(a, b, dims=NN):
    return lax.dot_general(a, b, dims, precision=EXACT, preferred_element_type=jnp.float32)


def dot16(a, b, dims=NN):
    return lax.dot_general(a, b, dims, preferred_element_type=jnp.float32)


def split(x):
    high = x.astype(jnp.bfloat16)
    return high, (x - high.astype(jnp.float32)).astype(jnp.bfloat16)


def dot3(a, b, dims=NN):
    return dot16(a[0], b[0], dims) + (dot16(a[0], b[1], dims) + dot16(a[1], b[0], dims))


class Sizes:
    def __init__(self, mesh, background, position, grade):
        self.n_state, self.n_mem = mesh.shape["state"], mesh.shape["mem"]
        self.rows = background.shape[0]
        self.unit = background.shape[1] // self.n_mem
        self.members = self.rows * self.n_mem
        self.batches, self.obs = position.shape
        self.blocks = grade.shape[2]
        self.width = self.unit // self.blocks
        self.whole = self.rows // SUBLANES * SUBLANES
        self.rest = self.rows - self.whole
        self.fold = self.whole // self.rest
        self.packed = self.unit + self.unit // self.fold
        self.tiles = self.batches * self.obs // LANES
        self.pairs = [(b, c) for c in range(self.batches) for b in range(c)]
        self.grade_rows = len(self.pairs) * self.blocks
        self.tail = self.obs - LANES
        assert self.batches * self.obs % LANES == 0 and 2 * self.tail == LANES
        assert self.rest and self.whole % self.rest == 0 and self.unit % (self.fold * self.width) == 0


def gather_kernel(z, owner_ref, pos_ref, bg_ref, grade_ref, p_ref, g_ref, slab, gbuf, sems, gsem):
    me_state, me_mem = lax.axis_index("state"), lax.axis_index("mem")
    me = me_state * z.n_mem + me_mem
    levels = pltpu.make_async_copy(grade_ref, gbuf, gsem)
    levels.start()

    def slab_copy(b):
        at = pl.multiple_of(lax.rem(owner_ref[b], z.n_mem) * z.unit, LANES)
        return pltpu.make_async_copy(bg_ref.at[:, pl.ds(at, z.unit)], slab.at[b], sems.at[b])

    here = [lax.div(owner_ref[b], z.n_mem) == me_state for b in range(z.batches)]
    for b in range(z.batches):
        pl.when(here[b])(lambda b=b: slab_copy(b).start())
    p_ref[...] = jnp.zeros_like(p_ref)
    levels.wait()
    for n, (b, c) in enumerate(z.pairs):
        mine = jnp.where(owner_ref[c] == me, 1.0, 0.0)
        g = gbuf[b].astype(jnp.float32) * mine
        g_ref[n * z.blocks:(n + 1) * z.blocks, :] = g[:, :LANES]
        half, r0 = n // (len(z.pairs) // 2), (n % (len(z.pairs) // 2)) * z.blocks + z.grade_rows
        g_ref[r0:r0 + z.blocks, half * z.tail:(half + 1) * z.tail] = g[:, LANES:]
    lane = lax.broadcasted_iota(jnp.int32, (z.rows, LANES), 1)

    def take(b):
        slab_copy(b).wait()
        first = b * z.obs
        while first < (b + 1) * z.obs:
            last = min((first // LANES + 1) * LANES, (b + 1) * z.obs)

            def body(q, acc):
                p = pos_ref[b, q - b * z.obs]
                at = pl.multiple_of(lax.div(p, LANES) * LANES, LANES)
                tile = slab[b, :, pl.ds(at, LANES)]
                to = lax.rem(q, LANES)
                tile = pltpu.roll(tile, lax.rem(to - p + at + LANES, LANES), 1)
                return jnp.where(lane == to, tile, acc)

            t = first // LANES
            acc = p_ref[t * z.rows:(t + 1) * z.rows, :]
            p_ref[t * z.rows:(t + 1) * z.rows, :] = lax.fori_loop(first, last, body, acc, unroll=16)
            first = last

    for b in range(z.batches):
        pl.when(here[b])(functools.partial(take, b))


def gather(z, owner, position, background, grade):
    return pl.pallas_call(
        functools.partial(gather_kernel, z),
        out_shape=(
            jax.ShapeDtypeStruct((z.tiles * z.rows, LANES), jnp.float32),
            jax.ShapeDtypeStruct((z.grade_rows * z.obs // LANES, LANES), jnp.float32),
        ),
        in_specs=[
            pl.BlockSpec(memory_space=pltpu.SMEM),
            pl.BlockSpec(memory_space=pltpu.SMEM),
            pl.BlockSpec(memory_space=pl.ANY),
            pl.BlockSpec(memory_space=pl.ANY),
        ],
        out_specs=(pl.BlockSpec(memory_space=pltpu.VMEM), pl.BlockSpec(memory_space=pltpu.VMEM)),
        scratch_shapes=[
            pltpu.VMEM((z.batches, z.rows, z.unit), jnp.float32),
            pltpu.VMEM(grade.shape, jnp.int32),
            pltpu.SemaphoreType.DMA((z.batches,)),
            pltpu.SemaphoreType.DMA,
        ],
        compiler_params=pltpu.CompilerParams(vmem_limit_bytes=VMEM_LIMIT),
        name="gather",
    )(owner, position, background, grade)


def pack_kernel(z, bg_ref, *refs):
    outs, rest, sem_w, sem_r = refs[:z.n_mem], refs[-3], refs[-2], refs[-1]
    me = lax.axis_index("mem")

    def copies(r):
        cols = pl.ds(pl.multiple_of(lax.bitwise_xor(me, r) * z.unit, LANES), z.unit)
        return (
            pltpu.make_async_copy(bg_ref.at[:z.whole, cols], outs[r].at[:, :z.unit], sem_w.at[r]),
            pltpu.make_async_copy(bg_ref.at[z.whole:, cols], rest.at[r], sem_r.at[r]),
        )

    order = list(range(1, z.n_mem)) + [0]
    for r in order:
        for copy in copies(r):
            copy.start()
    part = z.unit // z.fold
    for r in order:
        whole, tail = copies(r)
        tail.wait()
        for q in range(z.fold):
            outs[r][q * z.rest:(q + 1) * z.rest, z.unit:] = rest[r, :, q * part:(q + 1) * part]
        whole.wait()


def pack(z, background):
    shape = jax.ShapeDtypeStruct((z.whole, z.packed), jnp.float32)
    return pl.pallas_call(
        functools.partial(pack_kernel, z),
        out_shape=[shape] * z.n_mem,
        in_specs=[pl.BlockSpec(memory_space=pl.ANY)],
        out_specs=[pl.BlockSpec(memory_space=pltpu.VMEM)] * z.n_mem,
        scratch_shapes=[
            pltpu.VMEM((z.n_mem, z.rest, z.unit), jnp.float32),
            pltpu.SemaphoreType.DMA((z.n_mem,)),
            pltpu.SemaphoreType.DMA((z.n_mem,)),
        ],
        compiler_params=pltpu.CompilerParams(vmem_limit_bytes=VMEM_LIMIT),
        name="pack",
    )(background)


def serial_kernel(z, p_ref, g_ref, level_ref, y_ref, noise_ref, pos_ref, th_ref, tl_ref, pbuf, tbuf):
    n, scale = z.members, 1.0 / (z.members - 1)
    me = lax.axis_index("mem")
    for t in range(z.tiles):
        for m in range(z.n_mem):
            pbuf[m * z.rows:(m + 1) * z.rows, t * LANES:(t + 1) * LANES] = p_ref[m, t * z.rows:(t + 1) * z.rows, :]
    priors = [pbuf[:, b * z.obs:(b + 1) * z.obs] for b in range(z.batches)]
    row = lax.broadcasted_iota(jnp.int32, (n, n), 0)
    col = lax.broadcasted_iota(jnp.int32, (n, n), 1)
    eye = jnp.where(row == col, 1.0, 0.0)
    edge = z.whole * z.n_mem
    late = col >= edge
    source = jnp.where(late, lax.div(col - edge, z.rest), lax.div(col, z.whole))
    within = jnp.where(late, z.whole + lax.rem(col - edge, z.rest), lax.rem(col, z.whole))
    order = jnp.where(row == lax.bitwise_xor(source, me) * z.rows + within, 1.0, 0.0)
    block = lax.div(pos_ref[...], z.width)
    sub = lax.broadcasted_iota(jnp.int32, (z.blocks, z.obs), 0)
    pick = [jnp.where(sub == block[c:c + 1, :], 1.0, 0.0).astype(jnp.bfloat16) for c in range(z.batches)]

    def observed_levels(b, c):
        k = z.pairs.index((b, c))
        half, r0 = k // (len(z.pairs) // 2), (k % (len(z.pairs) // 2)) * z.blocks + z.grade_rows
        g = jnp.concatenate(
            [g_ref[k * z.blocks:(k + 1) * z.blocks, :], g_ref[r0:r0 + z.blocks, half * z.tail:(half + 1) * z.tail]], axis=1)
        return dot16(g.astype(jnp.bfloat16), pick[c], TN)

    for b in range(z.batches):
        prior = priors[b]
        mean = jnp.sum(prior, axis=0, keepdims=True) * (1.0 / n)
        spread = prior - mean
        innovation = y_ref[b:b + 1, :] - mean
        inv_noise = 1.0 / noise_ref[b:b + 1, :]
        weighted = spread * inv_noise
        gram = dot32(weighted, spread, NT) * scale
        shift = dot32(innovation, weighted, NT) * scale
        top = 1.0 + jnp.max(jnp.sum(jnp.abs(gram), axis=0, keepdims=True), axis=1, keepdims=True)
        first = 2.0 / (1.0 + top)
        e = (top - 1.0) / (top + 1.0)
        err = eye - first * (eye + gram)
        acc = first * (0.5 * eye + shift)

        def step(err, acc, e):
            both = dot32(jnp.concatenate([err, acc], axis=0), err)
            mu = 2.0 / (2.0 - e * e)
            return mu * both[:n] + (1.0 - mu) * eye, mu * (acc + both[n:]), e * e / (2.0 - e * e)

        for _ in range(4):
            err, acc, e = step(err, acc, e)
        err, acc, e = lax.while_loop(lambda s: jnp.max(s[2]) > 1e-3, lambda s: step(*s), (err, acc, e))
        acc = acc + dot32(acc, err)
        gain = innovation * inv_noise - dot32(acc, weighted)
        quarter = spread * (0.25 * scale)
        for c in range(b + 1, z.batches):
            priors[c] = priors[c] + dot32(gain, observed_levels(b, c) * dot32(quarter, priors[c], TN))
        right = split(dot32(order, quarter, TN) if b == 0 else quarter)

        def one_block(k, carry, b=b, gain=gain, right=right):
            left = split(gain * level_ref[b, pl.ds(k, 1), :].astype(jnp.float32))
            move = dot3(left, right, NT)
            if b == 0:
                new = order + move
            else:
                old = tbuf[k]
                new = old + dot3(split(move), split(old))
            if b + 1 < z.batches:
                tbuf[k] = new
            else:
                th_ref[k], tl_ref[k] = split(new)
            return carry

        lax.fori_loop(0, z.blocks, one_block, 0, unroll=4)


def serial(z, prior, grades, levels, readings, noise, position):
    out = jax.ShapeDtypeStruct((z.blocks, z.members, z.members), jnp.bfloat16)
    vmem = pl.BlockSpec(memory_space=pltpu.VMEM)
    return pl.pallas_call(
        functools.partial(serial_kernel, z),
        out_shape=(out, out),
        in_specs=[vmem] * 6,
        out_specs=(vmem, vmem),
        scratch_shapes=[
            pltpu.VMEM((z.members, z.tiles * LANES), jnp.float32),
            pltpu.VMEM((z.blocks, z.members, z.members), jnp.float32),
        ],
        compiler_params=pltpu.CompilerParams(vmem_limit_bytes=VMEM_LIMIT),
        name="serial",
    )(prior, grades, levels, readings, noise, position)


def apply_kernel(z, th_ref, tl_ref, *refs):
    ins, out_ref, buf, sems = refs[:z.n_mem], refs[z.n_mem], refs[-2], refs[-1]
    part = z.unit // z.fold
    per = part // z.width
    for q in range(z.fold):

        def one_block(i, carry, q=q):
            at = pl.multiple_of(i * z.width, LANES)
            wide = pl.ds(q * part + at, z.width)
            rest = pl.ds(z.unit + at, z.width)
            x = jnp.concatenate(
                [r[:, wide] for r in ins] + [r[q * z.rest:(q + 1) * z.rest, rest] for r in ins], axis=0)
            k = q * per + i
            buf[:, wide] = dot3((th_ref[k], tl_ref[k]), split(x))
            return carry

        lax.fori_loop(0, per, one_block, 0, unroll=2)
        cols = pl.ds(q * part, part)
        pltpu.make_async_copy(buf.at[:, cols], out_ref.at[:, cols], sems.at[q]).start()
    for q in range(z.fold):
        cols = pl.ds(q * part, part)
        pltpu.make_async_copy(buf.at[:, cols], out_ref.at[:, cols], sems.at[q]).wait()


def apply(z, moves, parts):
    vmem = pl.BlockSpec(memory_space=pltpu.VMEM)
    return pl.pallas_call(
        functools.partial(apply_kernel, z),
        out_shape=jax.ShapeDtypeStruct((z.members, z.unit), jnp.float32),
        in_specs=[vmem] * (2 + z.n_mem),
        out_specs=pl.BlockSpec(memory_space=pl.ANY),
        scratch_shapes=[
            pltpu.VMEM((z.members, z.unit), jnp.float32),
            pltpu.SemaphoreType.DMA((z.fold,)),
        ],
        compiler_params=pltpu.CompilerParams(vmem_limit_bytes=VMEM_LIMIT),
        name="apply",
    )(*moves, *parts)


def swap(x, axis, bit, size):
    return lax.ppermute(x, axis, [(i, i ^ bit) for i in range(size)])


def share(z, prior, grades):
    me = lax.axis_index("mem")
    half = grades.shape[0] // 2
    odd = me % 2 == 1
    low, high = grades[:half], grades[half:]
    mine = jnp.where(odd, high, low) + swap(jnp.where(odd, low, high), "mem", 1, z.n_mem)
    both = jnp.concatenate([prior, mine], axis=0)
    bit = 1
    while bit < z.n_state:
        both = both + swap(both, "state", bit, z.n_state)
        bit *= 2
    prior, mine = both[:prior.shape[0]], both[prior.shape[0]:]
    there = swap(both, "mem", 2, z.n_mem)
    other, mine = there[:prior.shape[0]], mine + there[prior.shape[0]:]
    upper = me >= 2
    pair = jnp.stack([jnp.where(upper, other, prior), jnp.where(upper, prior, other)])
    rows = pair.shape[0] * pair.shape[1]
    both = jnp.concatenate([pair.reshape(rows, LANES), mine], axis=0)
    there = swap(both, "mem", 1, z.n_mem)
    pair_t = there[:rows].reshape(pair.shape)
    mine_t = there[rows:]
    even, uneven = jnp.where(odd, pair_t, pair), jnp.where(odd, pair, pair_t)
    prior = jnp.stack([even[0], uneven[0], even[1], uneven[1]])
    grades = jnp.concatenate([jnp.where(odd, mine_t, mine), jnp.where(odd, mine, mine_t)], axis=0)
    return prior, grades


def solution(mesh):
    def local(background, readings, noise, owner, position, grade):
        z = Sizes(mesh, background, position, grade)
        levels = jnp.transpose(grade, (0, 2, 1))
        parts = pack(z, background)
        parts = [parts[0]] + [swap(parts[r], "mem", r, z.n_mem) for r in range(1, z.n_mem)]
        prior, grades = gather(z, owner, position, background, levels)
        prior, grades = share(z, prior, grades)
        moves = serial(z, prior, grades, levels, readings, noise, position)
        return apply(z, moves, parts)

    return jax.shard_map(
        local,
        mesh=mesh,
        in_specs=(P("mem", "state"), P(), P(), P(), P(), P(None, None, ("state", "mem"))),
        out_specs=P(None, ("state", "mem")),
        check_vma=False,
    )
```

time: 767 us -> 106 us (0.14)
  matrix products: 210 us -> 0 us
  other arithmetic: 198 us -> 5.08 us
  local copies, waits for them, and re-layouts: 172 us -> 0.04 us
  blocking collectives: 166 us -> 0 us
  Pallas kernels: 0 us -> 52.4 us
  waiting for transfers between devices: 0.01 us -> 36.9 us
  between operations: 9.04 us -> 0.1 us
    dot_general x24 -> x0, matrix products: 206 us -> none  [the longest x4 75.4 us: update_columns(): jnp.dot(spread.T, anomaly, precision=PRECISE)]
    another operation x46 -> x3, other arithmetic: 194 us -> 0.75 us  [the longest x1 0.73 us: share(): prior = jnp.stack([even[0], uneven[0], even[1], uneven[1]])]
    psum x4 -> x0, blocking collectives: 166 us -> none  [broadcast(): return lax.psum(block, axis)]
    unnamed x30 -> x4, local copies, waits for them, and re-layouts: 82.1 us -> 0.01 us
    pallas_call x0 -> x4, Pallas kernels: none -> 52.4 us  [the longest x1 33.9 us: serial(): pl.pallas_call(functools.partial(serial_kernel, z), out_shape=(out, out),...]
    ppermute x0 -> x9, waiting for transfers between devices: none -> 36.9 us  [swap(): return lax.ppermute(x, axis, [(i, i ^ bit) for i in range(size)])]
    all_to_all x4 -> x0, local copies, waits for them, and re-layouts: 27.8 us -> none  [local(): lax.all_to_all(background_matrix, 'mem', split_axis=1, concat_axis=0, til...]
    add x7 -> x0, local copies, waits for them, and re-layouts: 24.2 us -> none  [the longest x3 23.8 us: update_columns(): return center + anomaly]
  transfers between devices with their start and end apart: 1 -> 9, of which waited for: 0 -> 6; matrix products, arithmetic and copies ran while one was open for 14% -> 1% of each run, Pallas kernels for 0% -> 37%
where the time goes in v1:
time: 106 us; the launch traced here: 104 us
  Pallas kernels  52.4 us (49%)
  waiting for transfers between devices  36.9 us (35%)
  starting transfers between devices  9.73 us (9%)
  other arithmetic  5.08 us (5%)
    ppermute x9, waiting for transfers between devices, swap(): return lax.ppermute(x, axis, [(i, i ^ bit) for i in range(size)])  36.9 us
    pallas_call x1, Pallas kernels, serial(): pl.pallas_call(functools.partial(serial_kernel, z), out_shape=(out, out),...  33.9 us
    ppermute x9, starting transfers between devices, swap(): return lax.ppermute(x, axis, [(i, i ^ bit) for i in range(size)])  9.73 us
    pallas_call x1, Pallas kernels, apply(): pl.pallas_call(functools.partial(apply_kernel, z), out_shape=jax.ShapeDty...  8.31 us
    pallas_call x1, Pallas kernels, gather(): pl.pallas_call(functools.partial(gather_kernel, z), out_shape=(jax.ShapeD...  5.31 us
    pallas_call x1, Pallas kernels, pack(): pl.pallas_call(functools.partial(pack_kernel, z), out_shape=[shape] * z.n...  4.92 us
  transfers between devices with their start and end apart: 9, of which 6 were waited for; matrix products, arithmetic and copies ran while one was open for 1% of the time, Pallas kernels for 37%

profile of v1, /device:TPU:0, one launch (start us, length us, event | category | flops | bytes accessed | tf_op | source)
XLA Modules:
  0.0 104.3 jit_solution(18049904482096445199)
XLA Ops:
  0.0 5.3 %gather.1 = (f32[120,128]{1,0:T(8,128)}, f32[288,128]{1,0:T(8,128)}) custom-call(s32[4]{0:T(128)} %owner_ref.1, s32[4,192]{1,0:T(4,128)} %pos_ref.3, f32[20,65536]{1,0:T(8,128)} %bg_ref.3, s32[4,32,192]{2,1,0:T(8,128)} %bitcast.7), custom_call_target="tpu_custom_call" | custom-call | tf_op jit(solution)/shard_map/gather/pallas_call | solution.py:104
  5.3 0.9 slice_select_fusion.2
  6.2 0.6 collective-permute-start
  6.8 0.9 collective-permute-done
  7.7 0.9 select_add_fusion
  8.7 0.8 pad_maximum_fusion.3
  9.5 0.1 collective-permute-start.1
  9.6 5.8 %collective-permute-done.1 = f32[264,128]{1,0:T(8,128)S(1)} collective-permute-done((f32[264,128]{1,0:T(8,128)S(1)}, f32[264,128]{1,0:T(8,128)S(1)}, u32[]{:S(2)}, u32[]{:S(2)}) %collective-permute-start.1) | collective-permute-done | bytes 135200 | tf_op jit(solution)/shard_map/ppermute | solution.py:300
  15.4 0.8 fusion
  16.3 2.6 %collective-permute-start.2 = (f32[264,128]{1,0:T(8,128)S(1)}, f32[264,128]{1,0:T(8,128)S(1)}, u32[]{:S(2)}, u32[]{:S(2)}) collective-permute-start(f32[264,128]{1,0:T(8,128)S(1)} %fusion), channel_id=1, source_target_pairs={{0,8},{4,12},{8,0},{12,4},{16,24},{20,28},{24,16},{28,20},{1,9},{5... | collective-permute-start | bytes 405512 | tf_op jit(solution)/shard_map/ppermute | solution.py:300
  18.8 3.3 %collective-permute-done.2 = f32[264,128]{1,0:T(8,128)S(1)} collective-permute-done((f32[264,128]{1,0:T(8,128)S(1)}, f32[264,128]{1,0:T(8,128)S(1)}, u32[]{:S(2)}, u32[]{:S(2)}) %collective-permute-start.2) | collective-permute-done | bytes 135200 | tf_op jit(solution)/shard_map/ppermute | solution.py:300
  22.2 2.8 %collective-permute-start.3 = (f32[264,128]{1,0:T(8,128)S(1)}, f32[264,128]{1,0:T(8,128)S(1)}, u32[]{:S(2)}, u32[]{:S(2)}) collective-permute-start(f32[264,128]{1,0:T(8,128)S(1)} %add.22), channel_id=1, source_target_pairs={{0,16},{4,20},{8,24},{12,28},{16,0},{20,4},{24,8},{28,12},{1,17},{... | collective-permute-start | bytes 405512 | tf_op jit(solution)/shard_map/ppermute | solution.py:300
  25.0 5.5 %collective-permute-done.3 = f32[264,128]{1,0:T(8,128)S(1)} collective-permute-done((f32[264,128]{1,0:T(8,128)S(1)}, f32[264,128]{1,0:T(8,128)S(1)}, u32[]{:S(2)}, u32[]{:S(2)}) %collective-permute-start.3) | collective-permute-done | bytes 135200 | tf_op jit(solution)/shard_map/ppermute | solution.py:300
  30.5 1.4 %collective-permute-start.4 = (f32[264,128]{1,0:T(8,128)S(1)}, f32[264,128]{1,0:T(8,128)S(1)}, u32[]{:S(2)}, u32[]{:S(2)}) collective-permute-start(f32[264,128]{1,0:T(8,128)S(1)} %add.23), channel_id=1, source_target_pairs={{0,2},{1,3},{2,0},{3,1},{4,6},{5,7},{6,4},{7,5},{8,10},{9,11},{10,... | collective-permute-start | bytes 405512 | tf_op jit(solution)/shard_map/ppermute | solution.py:300
  31.9 4.9 %pack.1 = (f32[16,20480]{1,0:T(8,128)}, f32[16,20480]{1,0:T(8,128)}, f32[16,20480]{1,0:T(8,128)}, f32[16,20480]{1,0:T(8,128)}) custom-call(f32[20,65536]{1,0:T(8,128)} %bg_ref.3), custom_call_target="tpu_custom_call" | custom-call | tf_op jit(solution)/shard_map/pack/pallas_call | solution.py:154
  36.9 0.1 collective-permute-start.6
  36.9 0.8 collective-permute-start.7
  37.7 1.1 %collective-permute-start.8 = (f32[16,20480]{1,0:T(8,128)}, f32[16,20480]{1,0:T(8,128)}, u32[]{:S(2)}, u32[]{:S(2)}) collective-permute-start(f32[16,20480]{1,0:T(8,128)} %get-tuple-element.20), channel_id=1, source_target_pairs={{0,3},{1,2},{2,1},{3,0},{4,7},{5,6},{6,5},{7,4},{8,11},{9,10},{10,... | collective-permute-start | bytes 3932168 | tf_op jit(solution)/shard_map/ppermute | solution.py:300
  38.8 0.0 collective-permute-done.4
  38.9 0.4 collective-permute-start.5
  39.3 1.2 %collective-permute-done.5 = f32[384,128]{1,0:T(8,128)S(1)} collective-permute-done((f32[384,128]{1,0:T(8,128)S(1)}, f32[384,128]{1,0:T(8,128)S(1)}, u32[]{:S(2)}, u32[]{:S(2)}) %collective-permute-start.5) | collective-permute-done | bytes 196640 | tf_op jit(solution)/shard_map/ppermute | solution.py:300
  40.5 0.7 pad_maximum_fusion.2.g_ref
  41.2 0.7 pad_maximum_fusion.p_ref
  41.9 33.9 %serial.1 = (bf16[32,80,80]{2,1,0:T(8,128)(2,1)}, bf16[32,80,80]{2,1,0:T(8,128)(2,1)}) custom-call(f32[4,120,128]{2,1,0:T(8,128)} %pad_maximum_fusion.p_ref, f32[288,128]{1,0:T(8,128)} %pad_maximum_fusion.2.g_ref, s32[4,32,192]{2,1,0:T(8,128)} %bitcast.8, f32[4,192]{1,0:T(4,128)} %y_ref.1, f32[4,192]{1,0:T(4,128)} %noise_ref.1, s32[4,192]{1,0:T(4,128)} %pos_ref.3), custom_call_target="tpu_custom_call" | custom-call | tf_op jit(solution)/shard_map/serial/pallas_call | solution.py:245
  75.8 0.0 collective-permute-done.6.refs_1_
  75.8 0.0 copy-start
  75.8 0.0 collective-permute-done.7.refs_2_
  75.9 0.0 copy-start.1
  75.9 20.1 %collective-permute-done.8.refs_3_ = f32[16,20480]{1,0:T(8,128)} collective-permute-done((f32[16,20480]{1,0:T(8,128)}, f32[16,20480]{1,0:T(8,128)}, u32[]{:S(2)}, u32[]{:S(2)}) %collective-permute-start.8) | collective-permute-done | bytes 1310752 | tf_op jit(solution)/shard_map/ppermute | solution.py:300
  96.0 0.0 copy-done
  96.0 0.0 copy-done.1
  96.0 8.3 %apply.1 = f32[80,16384]{1,0:T(8,128)} custom-call(bf16[32,80,80]{2,1,0:T(8,128)(2,1)} %get-tuple-element.15.th_ref, bf16[32,80,80]{2,1,0:T(8,128)(2,1)} %get-tuple-element.16.tl_ref, f32[16,20480]{1,0:T(8,128)} %get-tuple-element.17.refs_0_, f32[16,20480]{1,0:T(8,128)} %copy-done, f32[16,20480]{1,0:T(8,128)} %copy-done.1, ...), custom_call_target="tpu_custom_call" | custom-call | tf_op jit(solution)/shard_map/apply/pallas_call | solution.py:285
  (10 shorter events, 0.2 us)
Async XLA Ops:
  6.2 1.5 %collective-permute-start = (f32[144,128]{1,0:T(8,128)S(1)}, f32[144,128]{1,0:T(8,128)S(1)}, u32[]{:S(2)}, u32[]{:S(2)}) collective-permute-start(f32[144,128]{1,0:T(8,128)S(1)} %slice_select_fusion.2), channel_id=1, source_target_pairs={{0,1},{1,0},{2,3},{3,2},{4,5},{5,4},{6,7},{7,6},{8,9},{9,8},{10,11... | collective-permute-start | bytes 221192 | tf_op jit(solution)/shard_map/ppermute | solution.py:300
  9.5 5.9 %collective-permute-start.1 = (f32[264,128]{1,0:T(8,128)S(1)}, f32[264,128]{1,0:T(8,128)S(1)}, u32[]{:S(2)}, u32[]{:S(2)}) collective-permute-start(f32[264,128]{1,0:T(8,128)S(1)} %pad_maximum_fusion.3), channel_id=1, source_target_pairs={{0,4},{4,0},{8,12},{12,8},{16,20},{20,16},{24,28},{28,24},{1,5},{5... | collective-permute-start | bytes 405512 | tf_op jit(solution)/shard_map/ppermute | solution.py:300
  16.3 5.9 %collective-permute-start.2 = (f32[264,128]{1,0:T(8,128)S(1)}, f32[264,128]{1,0:T(8,128)S(1)}, u32[]{:S(2)}, u32[]{:S(2)}) collective-permute-start(f32[264,128]{1,0:T(8,128)S(1)} %fusion), channel_id=1, source_target_pairs={{0,8},{4,12},{8,0},{12,4},{16,24},{20,28},{24,16},{28,20},{1,9},{5... | collective-permute-start | bytes 405512 | tf_op jit(solution)/shard_map/ppermute | solution.py:300
  22.2 8.4 %collective-permute-start.3 = (f32[264,128]{1,0:T(8,128)S(1)}, f32[264,128]{1,0:T(8,128)S(1)}, u32[]{:S(2)}, u32[]{:S(2)}) collective-permute-start(f32[264,128]{1,0:T(8,128)S(1)} %add.22), channel_id=1, source_target_pairs={{0,16},{4,20},{8,24},{12,28},{16,0},{20,4},{24,8},{28,12},{1,17},{... | collective-permute-start | bytes 405512 | tf_op jit(solution)/shard_map/ppermute | solution.py:300
  30.5 8.2 %collective-permute-start.4 = (f32[264,128]{1,0:T(8,128)S(1)}, f32[264,128]{1,0:T(8,128)S(1)}, u32[]{:S(2)}, u32[]{:S(2)}) collective-permute-start(f32[264,128]{1,0:T(8,128)S(1)} %add.23), channel_id=1, source_target_pairs={{0,2},{1,3},{2,0},{3,1},{4,6},{5,7},{6,4},{7,5},{8,10},{9,11},{10,... | collective-permute-start | bytes 405512 | tf_op jit(solution)/shard_map/ppermute | solution.py:300
  36.9 39.0 %collective-permute-start.6 = (f32[16,20480]{1,0:T(8,128)}, f32[16,20480]{1,0:T(8,128)S(1)}, u32[]{:S(2)}, u32[]{:S(2)}) collective-permute-start(f32[16,20480]{1,0:T(8,128)} %get-tuple-element.18), channel_id=1, source_target_pairs={{0,1},{1,0},{2,3},{3,2},{4,5},{5,4},{6,7},{7,6},{8,9},{9,8},{10,11... | collective-permute-start | bytes 3932168 | tf_op jit(solution)/shard_map/ppermute | solution.py:300
  36.9 38.9 %collective-permute-start.7 = (f32[16,20480]{1,0:T(8,128)}, f32[16,20480]{1,0:T(8,128)S(1)}, u32[]{:S(2)}, u32[]{:S(2)}) collective-permute-start(f32[16,20480]{1,0:T(8,128)} %get-tuple-element.19), channel_id=1, source_target_pairs={{0,2},{1,3},{2,0},{3,1},{4,6},{5,7},{6,4},{7,5},{8,10},{9,11},{10,... | collective-permute-start | bytes 3932168 | tf_op jit(solution)/shard_map/ppermute | solution.py:300
  37.7 58.3 %collective-permute-start.8 = (f32[16,20480]{1,0:T(8,128)}, f32[16,20480]{1,0:T(8,128)}, u32[]{:S(2)}, u32[]{:S(2)}) collective-permute-start(f32[16,20480]{1,0:T(8,128)} %get-tuple-element.20), channel_id=1, source_target_pairs={{0,3},{1,2},{2,1},{3,0},{4,7},{5,6},{6,5},{7,4},{8,11},{9,10},{10,... | collective-permute-start | bytes 3932168 | tf_op jit(solution)/shard_map/ppermute | solution.py:300
  38.9 1.6 %collective-permute-start.5 = (f32[384,128]{1,0:T(8,128)S(1)}, f32[384,128]{1,0:T(8,128)S(1)}, u32[]{:S(2)}, u32[]{:S(2)}) collective-permute-start(f32[384,128]{1,0:T(8,128)S(1)} %pad_maximum_fusion.1), channel_id=1, source_target_pairs={{0,1},{1,0},{2,3},{3,2},{4,5},{5,4},{6,7},{7,6},{8,9},{9,8},{10,11... | collective-permute-start | bytes 589832 | tf_op jit(solution)/shard_map/ppermute | solution.py:300
  75.8 20.1 %copy-start = (f32[16,20480]{1,0:T(8,128)}, f32[16,20480]{1,0:T(8,128)S(1)}, u32[]{:S(2)}) copy-start(f32[16,20480]{1,0:T(8,128)S(1)} %collective-permute-done.6.refs_1_) | copy-start | bytes 3932164
  75.9 20.1 %copy-start.1 = (f32[16,20480]{1,0:T(8,128)}, f32[16,20480]{1,0:T(8,128)S(1)}, u32[]{:S(2)}) copy-start(f32[16,20480]{1,0:T(8,128)S(1)} %collective-permute-done.7.refs_2_) | copy-start | bytes 3932164

commit v2 on v1

--- a/solution.py
+++ b/solution.py
@@ -7,13 +7,15 @@
 from jax.experimental.pallas import tpu as pltpu
 from jax.sharding import PartitionSpec as P
 
+
 LANES = 128
 SUBLANES = 8
 EXACT = lax.Precision.HIGHEST
 NN = (((1,), (0,)), ((), ()))
 NT = (((1,), (1,)), ((), ()))
 TN = (((0,), (0,)), ((), ()))
-VMEM_LIMIT = 56 * 1024 * 1024
+MIB = 1024 * 1024
+GROUP = 4
 
 
 def dot32(a, b, dims=NN):
@@ -120,7 +122,7 @@
             pltpu.SemaphoreType.DMA((z.batches,)),
             pltpu.SemaphoreType.DMA,
         ],
-        compiler_params=pltpu.CompilerParams(vmem_limit_bytes=VMEM_LIMIT),
+        compiler_params=pltpu.CompilerParams(vmem_limit_bytes=16 * MIB),
         name="gather",
     )(owner, position, background, grade)
 
@@ -150,7 +152,7 @@
 
 
 def pack(z, background):
-    shape = jax.ShapeDtypeStruct((z.whole, z.packed), jnp.float32)
+    shape = pltpu.VMEM((z.whole, z.packed), jnp.float32)
     return pl.pallas_call(
         functools.partial(pack_kernel, z),
         out_shape=[shape] * z.n_mem,
@@ -161,26 +163,34 @@
             pltpu.SemaphoreType.DMA((z.n_mem,)),
             pltpu.SemaphoreType.DMA((z.n_mem,)),
         ],
-        compiler_params=pltpu.CompilerParams(vmem_limit_bytes=VMEM_LIMIT),
+        compiler_params=pltpu.CompilerParams(vmem_limit_bytes=8 * MIB),
         name="pack",
     )(background)
 
 
-def serial_kernel(z, p_ref, g_ref, level_ref, y_ref, noise_ref, pos_ref, th_ref, tl_ref, pbuf, tbuf):
+def pair_lanes(x):
+    return jnp.concatenate(split(x), axis=1)
+
+
+def halves(x):
+    return x[:, :LANES] + x[:, LANES:]
+
+
+def serial_kernel(z, p_ref, g_ref, level_ref, y_ref, noise_ref, pos_ref, out_ref, pbuf, fbuf, tbuf, mbuf):
     n, scale = z.members, 1.0 / (z.members - 1)
     me = lax.axis_index("mem")
     for t in range(z.tiles):
         for m in range(z.n_mem):
             pbuf[m * z.rows:(m + 1) * z.rows, t * LANES:(t + 1) * LANES] = p_ref[m, t * z.rows:(t + 1) * z.rows, :]
     priors = [pbuf[:, b * z.obs:(b + 1) * z.obs] for b in range(z.batches)]
-    row = lax.broadcasted_iota(jnp.int32, (n, n), 0)
-    col = lax.broadcasted_iota(jnp.int32, (n, n), 1)
-    eye = jnp.where(row == col, 1.0, 0.0)
+    row = lax.broadcasted_iota(jnp.int32, (n, LANES), 0)
+    col = lax.broadcasted_iota(jnp.int32, (n, LANES), 1)
+    eye = jnp.where(row == col, 1.0, 0.0)[:, :n]
     edge = z.whole * z.n_mem
     late = col >= edge
     source = jnp.where(late, lax.div(col - edge, z.rest), lax.div(col, z.whole))
     within = jnp.where(late, z.whole + lax.rem(col - edge, z.rest), lax.rem(col, z.whole))
-    order = jnp.where(row == lax.bitwise_xor(source, me) * z.rows + within, 1.0, 0.0)
+    order = jnp.where((row == lax.bitwise_xor(source, me) * z.rows + within) & (col < n), 1.0, 0.0)
     block = lax.div(pos_ref[...], z.width)
     sub = lax.broadcasted_iota(jnp.int32, (z.blocks, z.obs), 0)
     pick = [jnp.where(sub == block[c:c + 1, :], 1.0, 0.0).astype(jnp.bfloat16) for c in range(z.batches)]
@@ -192,6 +202,64 @@
             [g_ref[k * z.blocks:(k + 1) * z.blocks, :], g_ref[r0:r0 + z.blocks, half * z.tail:(half + 1) * z.tail]], axis=1)
         return dot16(g.astype(jnp.bfloat16), pick[c], TN)
 
+    def newton(state):
+        err, acc, e = state
+        both = dot32(jnp.concatenate([err, acc], axis=0), err)
+        mu = 2.0 / (2.0 - e * e)
+        return mu * both[:n] + (1.0 - mu) * eye, mu * (acc + both[n:]), e * e / (2.0 - e * e)
+
+    def make_moves(b, i, gain, right):
+        left = []
+        for u in range(GROUP):
+            high, low = split(gain * level_ref[b, pl.ds(i * GROUP + u, 1), :].astype(jnp.float32))
+            left.append(jnp.concatenate([high, gap_lanes, low], axis=1))
+        both = dot16(jnp.concatenate(left, axis=0), right, NT)
+        for u in range(GROUP):
+            move = halves(both[n * u:n * (u + 1)])
+            if b == 0:
+                keep(b, i * GROUP + u, order + move)
+            else:
+                mbuf[lax.rem(i, 2), u] = pair_lanes(move)
+
+    def keep(b, k, new):
+        high, low = split(new)
+        if b + 1 < z.batches:
+            fbuf[k] = new
+            both = jnp.concatenate([high, low], axis=1)
+            tbuf[k, :n] = both
+            tbuf[k, LANES:] = both
+        else:
+            out_ref[k] = jnp.concatenate([high[:, :n], high[:, :n], low[:, :n]], axis=1)
+
+    def use_moves(b, i):
+        for u in range(GROUP):
+            k = i * GROUP + u
+            keep(b, k, fbuf[k] + halves(dot16(mbuf[lax.rem(i, 2), u][:, :LANES + n], tbuf[k])))
+
+    groups = z.blocks // GROUP
+
+    def blocks(b, gain, right, also, state):
+        if b == 0:
+
+            def body(i, state):
+                make_moves(b, i, gain, right)
+                return also(state)
+
+            return lax.fori_loop(0, groups, body, state)
+        make_moves(b, 0, gain, right)
+
+        def body(i, state):
+            use_moves(b, i)
+            make_moves(b, i + 1, gain, right)
+            return also(state)
+
+        state = lax.fori_loop(0, groups - 1, body, state)
+        use_moves(b, groups - 1)
+        return state
+
+    gap_lanes = jnp.zeros((n, 2 * LANES - z.obs), jnp.bfloat16)
+    tbuf[:, n:LANES, :] = jnp.zeros((z.blocks, LANES - n, 2 * LANES), jnp.bfloat16)
+    before = None
     for b in range(z.batches):
         prior = priors[b]
         mean = jnp.sum(prior, axis=0, keepdims=True) * (1.0 / n)
@@ -203,60 +271,48 @@
         shift = dot32(innovation, weighted, NT) * scale
         top = 1.0 + jnp.max(jnp.sum(jnp.abs(gram), axis=0, keepdims=True), axis=1, keepdims=True)
         first = 2.0 / (1.0 + top)
-        e = (top - 1.0) / (top + 1.0)
-        err = eye - first * (eye + gram)
-        acc = first * (0.5 * eye + shift)
-
-        def step(err, acc, e):
-            both = dot32(jnp.concatenate([err, acc], axis=0), err)
-            mu = 2.0 / (2.0 - e * e)
-            return mu * both[:n] + (1.0 - mu) * eye, mu * (acc + both[n:]), e * e / (2.0 - e * e)
-
-        for _ in range(4):
-            err, acc, e = step(err, acc, e)
-        err, acc, e = lax.while_loop(lambda s: jnp.max(s[2]) > 1e-3, lambda s: step(*s), (err, acc, e))
+        state = (eye - first * (eye + gram), first * (0.5 * eye + shift), (top - 1.0) / (top + 1.0))
+        if before is None:
+            for _ in range(4):
+                state = newton(state)
+        else:
+            state = blocks(*before, newton, state)
+        err, acc, _ = lax.while_loop(lambda s: jnp.max(s[2]) > 1e-3, newton, state)
         acc = acc + dot32(acc, err)
         gain = innovation * inv_noise - dot32(acc, weighted)
         quarter = spread * (0.25 * scale)
+        gain2, quarter2 = split(gain), split(quarter)
         for c in range(b + 1, z.batches):
-            priors[c] = priors[c] + dot32(gain, observed_levels(b, c) * dot32(quarter, priors[c], TN))
-        right = split(dot32(order, quarter, TN) if b == 0 else quarter)
-
-        def one_block(k, carry, b=b, gain=gain, right=right):
-            left = split(gain * level_ref[b, pl.ds(k, 1), :].astype(jnp.float32))
-            move = dot3(left, right, NT)
-            if b == 0:
-                new = order + move
-            else:
-                old = tbuf[k]
-                new = old + dot3(split(move), split(old))
-            if b + 1 < z.batches:
-                tbuf[k] = new
-            else:
-                th_ref[k], tl_ref[k] = split(new)
-            return carry
-
-        lax.fori_loop(0, z.blocks, one_block, 0, unroll=4)
+            change = split(observed_levels(b, c) * dot3(quarter2, split(priors[c]), TN))
+            priors[c] = priors[c] + dot3(gain2, change)
+        gap = jnp.zeros((LANES - n, z.obs), jnp.bfloat16)
+        high, low = split(dot32(order[:, :n], quarter, TN) if b == 0 else quarter)
+        right = jnp.concatenate([high, gap, low, gap], axis=0)
+        gap = jnp.zeros((2 * LANES, 2 * LANES - z.obs), jnp.bfloat16)
+        before = (b, gain, jnp.concatenate([right, gap, right], axis=1))
+
+    blocks(*before, lambda state: state, 0)
 
 
 def serial(z, prior, grades, levels, readings, noise, position):
-    out = jax.ShapeDtypeStruct((z.blocks, z.members, z.members), jnp.bfloat16)
     vmem = pl.BlockSpec(memory_space=pltpu.VMEM)
     return pl.pallas_call(
         functools.partial(serial_kernel, z),
-        out_shape=(out, out),
+        out_shape=jax.ShapeDtypeStruct((z.blocks, z.members, 3 * z.members), jnp.bfloat16),
         in_specs=[vmem] * 6,
-        out_specs=(vmem, vmem),
+        out_specs=vmem,
         scratch_shapes=[
             pltpu.VMEM((z.members, z.tiles * LANES), jnp.float32),
-            pltpu.VMEM((z.blocks, z.members, z.members), jnp.float32),
+            pltpu.VMEM((z.blocks, z.members, LANES), jnp.float32),
+            pltpu.VMEM((z.blocks, LANES + z.members, 2 * LANES), jnp.bfloat16),
+            pltpu.VMEM((2, GROUP, z.members, 2 * LANES), jnp.bfloat16),
         ],
-        compiler_params=pltpu.CompilerParams(vmem_limit_bytes=VMEM_LIMIT),
+        compiler_params=pltpu.CompilerParams(vmem_limit_bytes=20 * MIB),
         name="serial",
     )(prior, grades, levels, readings, noise, position)
 
 
-def apply_kernel(z, th_ref, tl_ref, *refs):
+def apply_kernel(z, move_ref, *refs):
     ins, out_ref, buf, sems = refs[:z.n_mem], refs[z.n_mem], refs[-2], refs[-1]
     part = z.unit // z.fold
     per = part // z.width
@@ -269,7 +325,8 @@
             x = jnp.concatenate(
                 [r[:, wide] for r in ins] + [r[q * z.rest:(q + 1) * z.rest, rest] for r in ins], axis=0)
             k = q * per + i
-            buf[:, wide] = dot3((th_ref[k], tl_ref[k]), split(x))
+            high, low = split(x)
+            buf[:, wide] = dot16(move_ref[k], jnp.concatenate([high, low, high], axis=0))
             return carry
 
         lax.fori_loop(0, per, one_block, 0, unroll=2)
@@ -285,15 +342,15 @@
     return pl.pallas_call(
         functools.partial(apply_kernel, z),
         out_shape=jax.ShapeDtypeStruct((z.members, z.unit), jnp.float32),
-        in_specs=[vmem] * (2 + z.n_mem),
+        in_specs=[vmem] * (1 + z.n_mem),
         out_specs=pl.BlockSpec(memory_space=pl.ANY),
         scratch_shapes=[
             pltpu.VMEM((z.members, z.unit), jnp.float32),
             pltpu.SemaphoreType.DMA((z.fold,)),
         ],
-        compiler_params=pltpu.CompilerParams(vmem_limit_bytes=VMEM_LIMIT),
+        compiler_params=pltpu.CompilerParams(vmem_limit_bytes=14 * MIB),
         name="apply",
-    )(*moves, *parts)
+    )(moves, *(pltpu.with_memory_space_constraint(x, pltpu.VMEM) for x in parts))
 
 
 def swap(x, axis, bit, size):
@@ -331,8 +388,9 @@
     def local(background, readings, noise, owner, position, grade):
         z = Sizes(mesh, background, position, grade)
         levels = jnp.transpose(grade, (0, 2, 1))
-        parts = pack(z, background)
-        parts = [parts[0]] + [swap(parts[r], "mem", r, z.n_mem) for r in range(1, z.n_mem)]
+        parts = list(pack(z, background))
+        for r in range(z.n_mem - 1, 0, -1):
+            parts[r] = swap(parts[r], "mem", r, z.n_mem)
         prior, grades = gather(z, owner, position, background, levels)
         prior, grades = share(z, prior, grades)
         moves = serial(z, prior, grades, levels, readings, noise, position)

time: 106 us -> 102 us (0.962); the launches traced: 104 us -> 102 us
  waiting for transfers between devices: 36.9 us -> 56.6 us
  Pallas kernels: 52.4 us -> 32.8 us
  local copies, waits for them, and re-layouts: 0.04 us -> 5.09 us
  other arithmetic: 5.08 us -> 0.23 us
  starting transfers between devices: 9.73 us -> 6.68 us
    ppermute x9, waiting for transfers between devices: 36.9 us -> 56.6 us  [swap(): return lax.ppermute(x, axis, [(i, i ^ bit) for i in range(size)])]
    pallas_call x1, Pallas kernels: 33.9 us -> 18.1 us  [serial(): pl.pallas_call(functools.partial(serial_kernel, z), out_shape=jax.ShapeDt...]
    unnamed x4 -> x18, local copies, waits for them, and re-layouts: 0.01 us -> 5.06 us
    ppermute x9, starting transfers between devices: 9.73 us -> 6.68 us  [swap(): return lax.ppermute(x, axis, [(i, i ^ bit) for i in range(size)])]
    pallas_call x1, Pallas kernels: 4.92 us -> 2.61 us  [pack(): pl.pallas_call(functools.partial(pack_kernel, z), out_shape=[shape] * z.n...]
    pallas_call x1, Pallas kernels: 8.31 us -> 6.22 us  [apply(): pl.pallas_call(functools.partial(apply_kernel, z), out_shape=jax.ShapeDty...]
  transfers between devices with their start and end apart: 9 -> 9, of which waited for: 6 -> 7; matrix products, arithmetic and copies ran while one was open for 1% -> 0% of each run, Pallas kernels for 37% -> 20%
where the time goes in v2:
time: 102 us
  waiting for transfers between devices  56.6 us (55%)
  Pallas kernels  32.8 us (32%)
  starting transfers between devices  6.68 us (7%)
  local copies, waits for them, and re-layouts  5.09 us (5%)
    ppermute x9, waiting for transfers between devices, swap(): return lax.ppermute(x, axis, [(i, i ^ bit) for i in range(size)])  56.6 us
    pallas_call x1, Pallas kernels, serial(): pl.pallas_call(functools.partial(serial_kernel, z), out_shape=jax.ShapeDt...  18.1 us
    ppermute x9, starting transfers between devices, swap(): return lax.ppermute(x, axis, [(i, i ^ bit) for i in range(size)])  6.68 us
    pallas_call x1, Pallas kernels, apply(): pl.pallas_call(functools.partial(apply_kernel, z), out_shape=jax.ShapeDty...  6.22 us
    pallas_call x1, Pallas kernels, gather(): pl.pallas_call(functools.partial(gather_kernel, z), out_shape=(jax.ShapeD...  5.85 us
    unnamed x18, local copies, waits for them, and re-layouts  5.06 us
    pallas_call x1, Pallas kernels, pack(): pl.pallas_call(functools.partial(pack_kernel, z), out_shape=[shape] * z.n...  2.61 us
  transfers between devices with their start and end apart: 9, of which 7 were waited for; matrix products, arithmetic and copies ran while one was open for 0% of the time, Pallas kernels for 20%

profile of v2, /device:TPU:0, one launch (start us, length us, event | category | flops | bytes accessed | tf_op | source)
XLA Modules:
  0.0 101.6 jit_solution(16405638427641115050)
XLA Ops:
  0.0 0.0 copy-start
  0.0 2.8 %copy-done = f32[20,65536]{1,0:T(8,128)S(1)} copy-done((f32[20,65536]{1,0:T(8,128)S(1)}, f32[20,65536]{1,0:T(8,128)}, u32[]{:S(2)}) %copy-start) | copy-done | bytes 5242904
  2.8 0.0 copy-start.2
  2.8 0.9 copy-done.2
  3.7 0.0 copy-start.4
  3.7 0.7 copy-done.4
  4.4 0.0 copy-start.8
  4.4 0.7 copy-done.8
  5.0 0.0 copy-start.1
  5.0 5.9 %gather.1 = (f32[120,128]{1,0:T(8,128)S(1)}, f32[288,128]{1,0:T(8,128)S(1)}) custom-call(s32[4]{0:T(128)S(1)} %copy-done.8, s32[4,192]{1,0:T(4,128)S(1)} %copy-done.4, f32[20,65536]{1,0:T(8,128)S(1)} %copy-done, s32[4,32,192]{2,1,0:T(8,128)S(1)} %bitcast.7), custom_call_target="tpu_custom_call" | custom-call | tf_op jit(solution)/shard_map/gather/pallas_call | solution.py:106
  10.9 0.6 collective-permute-start
  11.5 0.9 collective-permute-done
  12.4 0.1 collective-permute-start.1
  12.5 5.8 %collective-permute-done.1 = f32[264,128]{1,0:T(8,128)S(1)} collective-permute-done((f32[264,128]{1,0:T(8,128)S(1)}, f32[264,128]{1,0:T(8,128)S(1)}, u32[]{:S(2)}, u32[]{:S(2)}) %collective-permute-start.1) | collective-permute-done | bytes 135200 | tf_op jit(solution)/shard_map/ppermute | solution.py:357
  18.4 0.2 collective-permute-start.2
  18.5 4.9 %collective-permute-done.2 = f32[264,128]{1,0:T(8,128)S(1)} collective-permute-done((f32[264,128]{1,0:T(8,128)S(1)}, f32[264,128]{1,0:T(8,128)S(1)}, u32[]{:S(2)}, u32[]{:S(2)}) %collective-permute-start.2) | collective-permute-done | bytes 135200 | tf_op jit(solution)/shard_map/ppermute | solution.py:357
  23.5 1.1 %collective-permute-start.3 = (f32[264,128]{1,0:T(8,128)S(1)}, f32[264,128]{1,0:T(8,128)S(1)}, u32[]{:S(2)}, u32[]{:S(2)}) collective-permute-start(f32[264,128]{1,0:T(8,128)S(1)} %add.22), channel_id=1, source_target_pairs={{0,16},{4,20},{8,24},{12,28},{16,0},{20,4},{24,8},{28,12},{1,17},{... | collective-permute-start | bytes 405512 | tf_op jit(solution)/shard_map/ppermute | solution.py:357
  24.5 6.6 %collective-permute-done.3 = f32[264,128]{1,0:T(8,128)S(1)} collective-permute-done((f32[264,128]{1,0:T(8,128)S(1)}, f32[264,128]{1,0:T(8,128)S(1)}, u32[]{:S(2)}, u32[]{:S(2)}) %collective-permute-start.3) | collective-permute-done | bytes 135200 | tf_op jit(solution)/shard_map/ppermute | solution.py:357
  31.2 2.5 %collective-permute-start.4 = (f32[264,128]{1,0:T(8,128)S(1)}, f32[264,128]{1,0:T(8,128)S(1)}, u32[]{:S(2)}, u32[]{:S(2)}) collective-permute-start(f32[264,128]{1,0:T(8,128)S(1)} %add.23), channel_id=1, source_target_pairs={{0,2},{1,3},{2,0},{3,1},{4,6},{5,7},{6,4},{7,5},{8,10},{9,11},{10,... | collective-permute-start | bytes 405512 | tf_op jit(solution)/shard_map/ppermute | solution.py:357
  33.7 0.0 copy-done.1
  33.7 2.6 %pack.1 = (f32[16,20480]{1,0:T(8,128)S(1)}, f32[16,20480]{1,0:T(8,128)}, f32[16,20480]{1,0:T(8,128)}, f32[16,20480]{1,0:T(8,128)}) custom-call(f32[20,65536]{1,0:T(8,128)S(1)} %copy-done.1), custom_call_target="tpu_custom_call" | custom-call | tf_op jit(solution)/shard_map/pack/pallas_call | solution.py:156
  36.3 0.1 collective-permute-start.6
  36.4 0.1 collective-permute-start.7
  36.5 1.7 %collective-permute-start.8 = (f32[16,20480]{1,0:T(8,128)}, f32[16,20480]{1,0:T(8,128)}, u32[]{:S(2)}, u32[]{:S(2)}) collective-permute-start(f32[16,20480]{1,0:T(8,128)} %get-tuple-element.16), channel_id=1, source_target_pairs={{0,3},{1,2},{2,1},{3,0},{4,7},{5,6},{6,5},{7,4},{8,11},{9,10},{10,... | collective-permute-start | bytes 3932168 | tf_op jit(solution)/shard_map/ppermute | solution.py:357
  38.2 0.0 collective-permute-done.4
  38.3 0.0 copy-start.3
  38.3 0.0 copy-start.5
  38.3 0.0 copy-start.6
  38.3 0.0 copy-start.7
  38.3 0.4 collective-permute-start.5
  38.8 1.1 %collective-permute-done.5 = f32[384,128]{1,0:T(8,128)S(1)} collective-permute-done((f32[384,128]{1,0:T(8,128)S(1)}, f32[384,128]{1,0:T(8,128)S(1)}, u32[]{:S(2)}, u32[]{:S(2)}) %collective-permute-start.5) | collective-permute-done | bytes 196640 | tf_op jit(solution)/shard_map/ppermute | solution.py:357
  40.0 0.0 copy-done.3
  40.0 0.0 copy-done.5
  40.0 0.0 copy-done.6
  40.0 0.0 copy-done.7
  40.1 18.1 %serial.1.move_ref = bf16[32,80,240]{2,1,0:T(8,128)(2,1)S(1)} custom-call(f32[4,120,128]{2,1,0:T(8,128)S(1)} %pad_maximum_fusion.p_ref, f32[288,128]{1,0:T(8,128)S(1)} %pad_maximum_fusion.2.g_ref, s32[4,32,192]{2,1,0:T(8,128)S(1)} %bitcast.8, f32[4,192]{1,0:T(4,128)S(1)} %copy-done.6, f32[4,192]{1,0:T(4,128)S(1)} %copy-done.7, s32[4,192]{1,0:T(4,128)S(1)} %copy-done.5), custom_call_target="tpu_custom_call" | custom-call | tf_op jit(solution)/shard_map/serial/pallas_call | solution.py:299
  58.2 0.0 collective-permute-done.6.refs_1_
  58.2 10.2 %collective-permute-done.7.refs_2_ = f32[16,20480]{1,0:T(8,128)} collective-permute-done((f32[16,20480]{1,0:T(8,128)}, f32[16,20480]{1,0:T(8,128)}, u32[]{:S(2)}, u32[]{:S(2)}) %collective-permute-start.7) | collective-permute-done | bytes 1310752 | tf_op jit(solution)/shard_map/ppermute | solution.py:357
  68.4 27.0 %collective-permute-done.8.refs_3_ = f32[16,20480]{1,0:T(8,128)} collective-permute-done((f32[16,20480]{1,0:T(8,128)}, f32[16,20480]{1,0:T(8,128)}, u32[]{:S(2)}, u32[]{:S(2)}) %collective-permute-start.8) | collective-permute-done | bytes 1310752 | tf_op jit(solution)/shard_map/ppermute | solution.py:357
  95.4 6.2 %apply.1 = f32[80,16384]{1,0:T(8,128)} custom-call(bf16[32,80,240]{2,1,0:T(8,128)(2,1)S(1)} %serial.1.move_ref, f32[16,20480]{1,0:T(8,128)S(1)} %get-tuple-element.13.refs_0_, f32[16,20480]{1,0:T(8,128)S(1)} %collective-permute-done.6.refs_1_, f32[16,20480]{1,0:T(8,128)} %collective-permute-done.7.refs_2_, f32[16,20480]{1,0:T(8,128)} %collective-permute-done.8.refs_3_), custom_call_target="tpu_custom_call" | custom-call | tf_op jit(solution)/shard_map/apply/pallas_call | solution.py:342
  (16 shorter events, 0.3 us)
Async XLA Ops:
  0.0 2.8 %copy-start = (f32[20,65536]{1,0:T(8,128)S(1)}, f32[20,65536]{1,0:T(8,128)}, u32[]{:S(2)}) copy-start(f32[20,65536]{1,0:T(8,128)} %bg_ref.3) | copy-start | bytes 15728644
  2.8 0.9 copy-start.2
  3.7 0.7 copy-start.4
  4.4 0.7 copy-start.8
  5.0 28.6 %copy-start.1 = (f32[20,65536]{1,0:T(8,128)S(1)}, f32[20,65536]{1,0:T(8,128)}, u32[]{:S(2)}) copy-start(f32[20,65536]{1,0:T(8,128)} %bg_ref.3) | copy-start | bytes 15728644
  10.9 1.5 %collective-permute-start = (f32[144,128]{1,0:T(8,128)S(1)}, f32[144,128]{1,0:T(8,128)S(1)}, u32[]{:S(2)}, u32[]{:S(2)}) collective-permute-start(f32[144,128]{1,0:T(8,128)S(1)} %slice_select_fusion.2), channel_id=1, source_target_pairs={{0,1},{1,0},{2,3},{3,2},{4,5},{5,4},{6,7},{7,6},{8,9},{9,8},{10,11... | collective-permute-start | bytes 221192 | tf_op jit(solution)/shard_map/ppermute | solution.py:357
  12.4 5.9 %collective-permute-start.1 = (f32[264,128]{1,0:T(8,128)S(1)}, f32[264,128]{1,0:T(8,128)S(1)}, u32[]{:S(2)}, u32[]{:S(2)}) collective-permute-start(f32[264,128]{1,0:T(8,128)S(1)} %pad_maximum_fusion.3), channel_id=1, source_target_pairs={{0,4},{4,0},{8,12},{12,8},{16,20},{20,16},{24,28},{28,24},{1,5},{5... | collective-permute-start | bytes 405512 | tf_op jit(solution)/shard_map/ppermute | solution.py:357
  18.4 5.1 %collective-permute-start.2 = (f32[264,128]{1,0:T(8,128)S(1)}, f32[264,128]{1,0:T(8,128)S(1)}, u32[]{:S(2)}, u32[]{:S(2)}) collective-permute-start(f32[264,128]{1,0:T(8,128)S(1)} %fusion), channel_id=1, source_target_pairs={{0,8},{4,12},{8,0},{12,4},{16,24},{20,28},{24,16},{28,20},{1,9},{5... | collective-permute-start | bytes 405512 | tf_op jit(solution)/shard_map/ppermute | solution.py:357
  23.5 7.7 %collective-permute-start.3 = (f32[264,128]{1,0:T(8,128)S(1)}, f32[264,128]{1,0:T(8,128)S(1)}, u32[]{:S(2)}, u32[]{:S(2)}) collective-permute-start(f32[264,128]{1,0:T(8,128)S(1)} %add.22), channel_id=1, source_target_pairs={{0,16},{4,20},{8,24},{12,28},{16,0},{20,4},{24,8},{28,12},{1,17},{... | collective-permute-start | bytes 405512 | tf_op jit(solution)/shard_map/ppermute | solution.py:357
  31.2 7.0 %collective-permute-start.4 = (f32[264,128]{1,0:T(8,128)S(1)}, f32[264,128]{1,0:T(8,128)S(1)}, u32[]{:S(2)}, u32[]{:S(2)}) collective-permute-start(f32[264,128]{1,0:T(8,128)S(1)} %add.23), channel_id=1, source_target_pairs={{0,2},{1,3},{2,0},{3,1},{4,6},{5,7},{6,4},{7,5},{8,10},{9,11},{10,... | collective-permute-start | bytes 405512 | tf_op jit(solution)/shard_map/ppermute | solution.py:357
  36.3 21.9 %collective-permute-start.6 = (f32[16,20480]{1,0:T(8,128)}, f32[16,20480]{1,0:T(8,128)S(1)}, u32[]{:S(2)}, u32[]{:S(2)}) collective-permute-start(f32[16,20480]{1,0:T(8,128)} %get-tuple-element.14), channel_id=1, source_target_pairs={{0,1},{1,0},{2,3},{3,2},{4,5},{5,4},{6,7},{7,6},{8,9},{9,8},{10,11... | collective-permute-start | bytes 3932168 | tf_op jit(solution)/shard_map/ppermute | solution.py:357
  36.4 32.0 %collective-permute-start.7 = (f32[16,20480]{1,0:T(8,128)}, f32[16,20480]{1,0:T(8,128)}, u32[]{:S(2)}, u32[]{:S(2)}) collective-permute-start(f32[16,20480]{1,0:T(8,128)} %get-tuple-element.15), channel_id=1, source_target_pairs={{0,2},{1,3},{2,0},{3,1},{4,6},{5,7},{6,4},{7,5},{8,10},{9,11},{10,... | collective-permute-start | bytes 3932168 | tf_op jit(solution)/shard_map/ppermute | solution.py:357
  36.5 58.9 %collective-permute-start.8 = (f32[16,20480]{1,0:T(8,128)}, f32[16,20480]{1,0:T(8,128)}, u32[]{:S(2)}, u32[]{:S(2)}) collective-permute-start(f32[16,20480]{1,0:T(8,128)} %get-tuple-element.16), channel_id=1, source_target_pairs={{0,3},{1,2},{2,1},{3,0},{4,7},{5,6},{6,5},{7,4},{8,11},{9,10},{10,... | collective-permute-start | bytes 3932168 | tf_op jit(solution)/shard_map/ppermute | solution.py:357
  38.3 1.7 %copy-start.3 = (s32[4,192,32]{1,2,0:T(8,128)S(1)}, s32[4,192,32]{1,2,0:T(8,128)}, u32[]{:S(2)}) copy-start(s32[4,192,32]{1,2,0:T(8,128)} %param.11) | copy-start | bytes 294916
  38.3 1.7 %copy-start.5 = (s32[4,192]{1,0:T(4,128)S(1)}, s32[4,192]{1,0:T(4,128)}, u32[]{:S(2)}) copy-start(s32[4,192]{1,0:T(4,128)} %pos_ref.3) | copy-start | bytes 9220
  38.3 1.7 %copy-start.6 = (f32[4,192]{1,0:T(4,128)S(1)}, f32[4,192]{1,0:T(4,128)}, u32[]{:S(2)}) copy-start(f32[4,192]{1,0:T(4,128)} %y_ref.1) | copy-start | bytes 9220
  38.3 1.7 %copy-start.7 = (f32[4,192]{1,0:T(4,128)S(1)}, f32[4,192]{1,0:T(4,128)}, u32[]{:S(2)}) copy-start(f32[4,192]{1,0:T(4,128)} %noise_ref.1) | copy-start | bytes 9220
  38.3 1.5 %collective-permute-start.5 = (f32[384,128]{1,0:T(8,128)S(1)}, f32[384,128]{1,0:T(8,128)S(1)}, u32[]{:S(2)}, u32[]{:S(2)}) collective-permute-start(f32[384,128]{1,0:T(8,128)S(1)} %pad_maximum_fusion.1), channel_id=1, source_target_pairs={{0,1},{1,0},{2,3},{3,2},{4,5},{5,4},{6,7},{7,6},{8,9},{9,8},{10,11... | collective-permute-start | bytes 589832 | tf_op jit(solution)/shard_map/ppermute | solution.py:357
